TPU v7x, 256 devices: a whole 4x4x8 slice. The times are simulated.
256 devices in a mesh: replica: 8 (over x, core), outer: 4 (over y), link: 8 (over z).
Axes of the slice: x: 4, y: 4, z: 8, core: 2. Of those that a mesh axis runs over, the one named last changes fastest.
Arguments:
- link_in: bfloat16 [8, 16384, 256], P('replica', ('outer', 'link')), may hold values from -6 to 6
- path_in: bfloat16 [8, 4096, 256], P('replica', ('outer', 'link')), may hold values from -6 to 6
- hop_slots: int32 [8, 4096, 24], P('replica', ('outer', 'link')), may hold values from 0 to 2047
- hop_lens: int32 [8, 4096], P('replica', ('outer', 'link')), may hold values from 2 to 24
- failed: int32 [8, 16384], P('replica', ('outer', 'link')), may hold values 0 or 1
- serve_index: int32 [8, 32, 32, 64], P('replica', None, ('outer', 'link')), may hold values from 0 to 511
- link_grad: bfloat16 [8, 16384, 256], P('replica', ('outer', 'link')), may hold values from -6 to 6
- path_grad: bfloat16 [8, 4096, 256], P('replica', ('outer', 'link')), may hold values from -6 to 6
- gru_wx: bfloat16 [256, 768], replicated, may hold values from -0.375 to 0.375
- gru_wh: bfloat16 [256, 768], replicated, may hold values from -0.375 to 0.375
- gru_bias: float32 [768], replicated, may hold values from -3 to 3
- mlp_w1: bfloat16 [512, 256], replicated, may hold values from -0.25 to 0.25
- mlp_b1: float32 [256], replicated, may hold values from -3 to 3
- mlp_w2: bfloat16 [256, 256], replicated, may hold values from -0.375 to 0.375
- mlp_b2: float32 [256], replicated, may hold values from -3 to 3
Outputs:
- link_out: bfloat16 [8, 16384, 256], P('replica', ('outer', 'link'))
- path_out: bfloat16 [8, 4096, 256], P('replica', ('outer', 'link'))
- link_in_grad: float32 [8, 16384, 256], P('replica', ('outer', 'link'))
- path_in_grad: float32 [8, 4096, 256], P('replica', ('outer', 'link'))
- grad_wx: float32 [256, 768], replicated
- grad_wh: float32 [256, 768], replicated
- grad_bias: float32 [768], replicated
- grad_w1: float32 [512, 256], replicated
- grad_b1: float32 [256], replicated
- grad_w2: float32 [256, 256], replicated
- grad_b2: float32 [256], replicated
Inputs may be any that keep to these rules, and one draw needn't show every extreme that they name: `serve_index`: entry [s, d, o, c] names, among the 512 links of owner device o, the link in request slot c of device d; a link may fill several slots. `hop_slots`: slot o * 64 + c is request slot c of the flow's own device towards owner o; entries at hops past the flow's length are ignored. 1 marks a failed link.
All inputs are finite; a program needn't handle non-finite values. No bound on the sum of `failed` on one device may be relied on, other than what follows from the above.
Results may differ from a plain program's by a relative error of at most 0.0067.
Values may be sent and summed in bfloat16 or wider, within the bound.
No kernel may reach another device: no remote copies, remote signals or barrier semaphores. Data moves between devices by JAX's collectives and lax.ppermute only.
A program may use at most 128 MiB of HBM per device.

v0:
```python
import jax
import jax.numpy as jnp
from jax import lax
from jax.sharding import PartitionSpec as P


def gate_terms(state_now, hop_input, input_weight, hidden_weight, gate_bias):
    from_input = jnp.dot(hop_input, input_weight, preferred_element_type=jnp.float32) + gate_bias
    from_state = jnp.dot(
        state_now.astype(jnp.bfloat16), hidden_weight, preferred_element_type=jnp.float32
    )
    return (from_input, from_state)


def gru_cell(state_now, from_input, from_state):
    feat_width = state_now.shape[1]
    update = jax.nn.sigmoid(from_input[:, :feat_width] + from_state[:, :feat_width])
    reset = jax.nn.sigmoid(
        from_input[:, feat_width : 2 * feat_width] + from_state[:, feat_width : 2 * feat_width]
    )
    candidate = jnp.tanh(from_input[:, 2 * feat_width :] + reset * from_state[:, 2 * feat_width :])
    return (candidate + update * (state_now - candidate), update, reset, candidate)


def gru_forward(path_start, hop_inputs, live_mask, input_weight, hidden_weight, gate_bias):

    def advance(state_now, scan_item):
        hop_input, live_now = scan_item
        from_input, from_state = gate_terms(
            state_now, hop_input, input_weight, hidden_weight, gate_bias
        )
        stepped = gru_cell(state_now, from_input, from_state)[0]
        state_next = jnp.where(live_now[:, None] > 0, stepped, state_now)
        return (state_next, (state_next,))

    return lax.scan(advance, path_start.astype(jnp.float32), (hop_inputs, live_mask))[1]


def back_step(
    carried, hop_input, state_now, live_now, hop_grad, from_input, from_state, input_tr, hidden_tr
):
    grad_state, grad_wx, grad_wh, grad_bias = carried
    feat_width = state_now.shape[1]
    live_col = live_now[:, None]
    grad_state = grad_state + live_col * hop_grad
    update, reset, candidate = gru_cell(state_now, from_input, from_state)[1:]
    pre_update = grad_state * (state_now - candidate) * update * (1.0 - update)
    pre_cand = grad_state * (1.0 - update) * (1.0 - candidate * candidate)
    pre_reset = pre_cand * from_state[:, 2 * feat_width :] * reset * (1.0 - reset)
    grad_in = jnp.concatenate([pre_update, pre_reset, pre_cand], axis=1) * live_col
    grad_hid = jnp.concatenate([pre_update, pre_reset, pre_cand * reset], axis=1) * live_col
    in_bf = grad_in.astype(jnp.bfloat16)
    hid_bf = grad_hid.astype(jnp.bfloat16)
    grad_prev = jnp.where(
        live_col > 0,
        grad_state * update + jnp.dot(hid_bf, hidden_tr, preferred_element_type=jnp.float32),
        grad_state,
    )
    grad_input = jnp.dot(in_bf, input_tr, preferred_element_type=jnp.float32)
    grad_wx = grad_wx + jnp.dot(hop_input.T, in_bf, preferred_element_type=jnp.float32)
    grad_wh = grad_wh + jnp.dot(
        state_now.astype(jnp.bfloat16).T, hid_bf, preferred_element_type=jnp.float32
    )
    grad_bias = grad_bias + jnp.sum(grad_in, axis=0)
    return ((grad_prev, grad_wx, grad_wh, grad_bias), grad_input)


def gru_backward(
    path_start,
    states,
    hop_inputs,
    live_mask,
    hop_grads,
    path_grad,
    input_weight,
    hidden_weight,
    gate_bias,
):
    feat_width = path_start.shape[1]
    prior_states = jnp.concatenate([path_start.astype(jnp.float32)[None], states[:-1]], axis=0)
    input_tr = input_weight.T
    hidden_tr = hidden_weight.T
    initial = (
        path_grad.astype(jnp.float32),
        jnp.zeros((feat_width, 3 * feat_width), jnp.float32),
        jnp.zeros((feat_width, 3 * feat_width), jnp.float32),
        jnp.zeros((3 * feat_width,), jnp.float32),
    )

    def retreat(carried, scan_item):
        hop_input, state_now, live_now, hop_grad = scan_item
        from_input, from_state = gate_terms(
            state_now, hop_input, input_weight, hidden_weight, gate_bias
        )
        return back_step(
            carried,
            hop_input,
            state_now,
            live_now,
            hop_grad,
            from_input,
            from_state,
            input_tr,
            hidden_tr,
        )

    scan_items = (hop_inputs, prior_states, live_mask, hop_grads)
    return lax.scan(retreat, initial, scan_items, reverse=True)


def link_forward(link_rows, agg_bf, keep_col, mlp_w1, mlp_b1, mlp_w2, mlp_b2):
    feat_width = link_rows.shape[1]
    pre_act = (
        jnp.dot(link_rows, mlp_w1[:feat_width], preferred_element_type=jnp.float32)
        + jnp.dot(agg_bf, mlp_w1[feat_width:], preferred_element_type=jnp.float32)
        + mlp_b1
    )
    activ = jax.nn.silu(pre_act).astype(jnp.bfloat16)
    value = (
        link_rows.astype(jnp.float32)
        + jnp.dot(activ, mlp_w2, preferred_element_type=jnp.float32)
        + mlp_b2
    )
    return ((keep_col * value).astype(jnp.bfloat16), pre_act, activ)


def link_backward(link_grad_rows, link_rows, agg_bf, keep_col, pre_act, activ, mlp_w1, mlp_w2):
    feat_width = link_rows.shape[1]
    grad_val = keep_col * link_grad_rows.astype(jnp.float32)
    val_bf = grad_val.astype(jnp.bfloat16)
    grad_w2 = jnp.dot(activ.T, val_bf, preferred_element_type=jnp.float32)
    grad_b2 = jnp.sum(grad_val, axis=0)
    grad_act = jnp.dot(val_bf, mlp_w2.T, preferred_element_type=jnp.float32)
    sigma = jax.nn.sigmoid(pre_act)
    grad_pre = grad_act * sigma * (1.0 + pre_act * (1.0 - sigma))
    pre_bf = grad_pre.astype(jnp.bfloat16)
    grad_w1 = jnp.concatenate(
        [
            jnp.dot(link_rows.T, pre_bf, preferred_element_type=jnp.float32),
            jnp.dot(agg_bf.T, pre_bf, preferred_element_type=jnp.float32),
        ],
        axis=0,
    )
    grad_b1 = jnp.sum(grad_pre, axis=0)
    link_direct = grad_val + jnp.dot(
        pre_bf, mlp_w1[:feat_width].T, preferred_element_type=jnp.float32
    )
    agg_grad = jnp.dot(pre_bf, mlp_w1[feat_width:].T, preferred_element_type=jnp.float32).astype(
        jnp.bfloat16
    )
    return (link_direct, agg_grad, (grad_w1, grad_b1, grad_w2, grad_b2))


def swap_slots(blocks):
    return lax.all_to_all(blocks, ("outer", "link"), split_axis=0, concat_axis=0, tiled=True)


def body(
    link_in,
    path_in,
    hop_slots,
    hop_lens,
    failed,
    serve_index,
    link_grad,
    path_grad,
    gru_wx,
    gru_wh,
    gru_bias,
    mlp_w1,
    mlp_b1,
    mlp_w2,
    mlp_b2,
):
    link_rows = link_in[0]
    feat_width = link_rows.shape[1]
    link_count = link_rows.shape[0]
    serve_rows = serve_index[0, :, 0, :]
    group_size, slot_cap = serve_rows.shape
    serve_flat = serve_rows.reshape(-1)
    slot_ids = hop_slots[0].T
    hop_count, flow_count = slot_ids.shape
    flat_slots = slot_ids.reshape(-1)
    live_mask = (jnp.arange(hop_count, dtype=jnp.int32)[:, None] < hop_lens[0][None, :]).astype(
        jnp.float32
    )
    fetched = swap_slots(jnp.take(link_rows, serve_rows, axis=0))
    hop_inputs = jnp.take(fetched.reshape(group_size * slot_cap, feat_width), slot_ids, axis=0)
    states = gru_forward(path_in[0], hop_inputs, live_mask, gru_wx, gru_wh, gru_bias)[0]
    partial_value = jax.ops.segment_sum(
        (states * live_mask[:, :, None]).reshape(hop_count * flow_count, feat_width),
        flat_slots,
        num_segments=group_size * slot_cap,
    ).astype(jnp.bfloat16)
    arrived = swap_slots(partial_value.reshape(group_size, slot_cap, feat_width))
    aggregate = jax.ops.segment_sum(
        arrived.reshape(group_size * slot_cap, feat_width).astype(jnp.float32),
        serve_flat,
        num_segments=link_count,
    )
    agg_bf = aggregate.astype(jnp.bfloat16)
    keep_col = (1 - failed[0]).astype(jnp.float32)[:, None]
    link_out, pre_act, activ = link_forward(
        link_rows, agg_bf, keep_col, mlp_w1, mlp_b1, mlp_w2, mlp_b2
    )
    path_out = states[-1].astype(jnp.bfloat16)
    link_direct, agg_grad, mlp_terms = link_backward(
        link_grad[0], link_rows, agg_bf, keep_col, pre_act, activ, mlp_w1, mlp_w2
    )
    returned = swap_slots(jnp.take(agg_grad, serve_rows, axis=0))
    hop_grads = (
        jnp.take(returned.reshape(group_size * slot_cap, feat_width), slot_ids, axis=0).astype(
            jnp.float32
        )
        * live_mask[:, :, None]
    )
    finished, grad_inputs = gru_backward(
        path_in[0], states, hop_inputs, live_mask, hop_grads, path_grad[0], gru_wx, gru_wh, gru_bias
    )
    dpart = jax.ops.segment_sum(
        grad_inputs.reshape(hop_count * flow_count, feat_width),
        flat_slots,
        num_segments=group_size * slot_cap,
    ).astype(jnp.bfloat16)
    owned = swap_slots(dpart.reshape(group_size, slot_cap, feat_width))
    link_back = link_direct + jax.ops.segment_sum(
        owned.reshape(group_size * slot_cap, feat_width).astype(jnp.float32),
        serve_flat,
        num_segments=link_count,
    )
    summed = lax.psum(
        (
            finished[1],
            finished[2],
            finished[3],
            mlp_terms[0],
            mlp_terms[1],
            mlp_terms[2],
            mlp_terms[3],
        ),
        ("replica", "outer", "link"),
    )
    device_count = lax.axis_size("replica") * lax.axis_size("outer") * lax.axis_size("link")
    grad_scale = float(device_count * link_count) ** (-0.5)
    return (
        link_out[None],
        path_out[None],
        link_back[None],
        finished[0][None],
        summed[0] * grad_scale,
        summed[1] * grad_scale,
        summed[2] * grad_scale,
        summed[3] * grad_scale,
        summed[4] * grad_scale,
        summed[5] * grad_scale,
        summed[6] * grad_scale,
    )


def solution(mesh):
    return jax.shard_map(
        body,
        mesh=mesh,
        in_specs=(
            P("replica", ("outer", "link"), None),
            P("replica", ("outer", "link"), None),
            P("replica", ("outer", "link"), None),
            P("replica", ("outer", "link")),
            P("replica", ("outer", "link")),
            P("replica", None, ("outer", "link"), None),
            P("replica", ("outer", "link"), None),
            P("replica", ("outer", "link"), None),
            P(),
            P(),
            P(),
            P(),
            P(),
            P(),
            P(),
        ),
        out_specs=(
            P("replica", ("outer", "link"), None),
            P("replica", ("outer", "link"), None),
            P("replica", ("outer", "link"), None),
            P("replica", ("outer", "link"), None),
            P(),
            P(),
            P(),
            P(),
            P(),
            P(),
            P(),
        ),
        check_vma=False,
    )
```

profile of v0, /device:TPU:2, one launch (start us, length us, event | category | flops | bytes accessed | tf_op | source)
XLA Modules:
  0.0 706.7 jit_solution(12861078215785412026)
XLA Ops:
  8.8 7.6 %gather_fusion = bf16[2048,256]{1,0:T(8,128)(2,1)S(1)} fusion(bf16[512,256]{1,0:T(8,128)(2,1)} %bitcast.135, s32[2048]{0:T(1024)S(1)} %broadcast_clamp_fusion), kind=kCustom, calls=%fused_computation.clone | custom fusion | bytes 2105344 | tf_op jit(solution)/shard_map/jit(_take)/gather | solution.py:187
  17.7 11.5 %all-to-all-start = ((bf16[32,64,256]{2,1,0:T(8,128)(2,1)}), bf16[32,64,256]{2,1,0:T(8,128)(2,1)S(1)}, u32[]{:S(2)}, u32[]{:S(2)}) async-start(bf16[32,64,256]{2,1,0:T(8,128)(2,1)} %broadcast_select_fusion.2), calls=%async_computation | async-start | bytes 2097152 | tf_op jit(solution)/shard_map/all_to_all | solution.py:155
  29.9 27.9 %all-to-all-done = bf16[32,64,256]{2,1,0:T(8,128)(2,1)S(1)} async-done(((bf16[32,64,256]{2,1,0:T(8,128)(2,1)}), bf16[32,64,256]{2,1,0:T(8,128)(2,1)S(1)}, u32[]{:S(2)}, u32[]{:S(2)}) %all-to-all-start) | async-done | bytes 1048608 | tf_op jit(solution)/shard_map/all_to_all | solution.py:155
  57.8 13.0 %gather_fusion.1 = bf16[3072,256]{1,0:T(8,128)(2,1)} fusion(bf16[2048,256]{1,0:T(8,128)(2,1)S(1)} %bitcast.137, s32[3072]{0:T(1024)S(1)} %bitcast_clamp_fusion), kind=kCustom, calls=%fused_computation.1.clone | custom fusion | bytes 3158016 | tf_op jit(solution)/shard_map/jit(_take)/gather | solution.py:188
  70.7 1.7 broadcast_select_fusion
  72.5 2.0 broadcast.84.clone
  74.6 29.4 %while.35 = (s32[]{:T(128)}, f32[128,256]{1,0:T(8,128)S(1)}, f32[24,128,256]{2,1,0:T(8,128)}, f32[24,128]{1,0:T(8,128)S(1)}, bf16[24,128,256]{2,1,0:T(8,128)(2,1...) while((s32[]{:T(128)}, f32[128,256]{1,0:T(8,128)S(1)}, ...), condition=%wide.region_1.4_spmd, body=%wide.region_0.3_spmd.sunk | while | flops 101253248 | bytes 2954097 | solution.py:36
  104.0 4.6 broadcast_multiply_fusion
  108.5 17.9 %scatter_custom_fusion = f32[2048,256]{1,0:T(8,128)S(1)} fusion(s32[3072]{0:T(1024)S(1)} %bitcast.155, f32[3072,256]{1,0:T(8,128)} %bitcast.148, f32[]{:T(128)} %constant.108.clone.1), kind=kCustom, calls=%fused_computation.102 | custom fusion | flops 786432 | bytes 2097664 | tf_op jit(solution)/shard_map/scatter-add | solution.py:190
  127.6 5.2 all-to-all-start.1
  135.5 25.6 %all-to-all-done.1 = bf16[32,64,256]{2,1,0:T(8,128)(2,1)S(1)} async-done(((bf16[32,64,256]{2,1,0:T(8,128)(2,1)}), bf16[32,64,256]{2,1,0:T(8,128)(2,1)S(1)}, u32[]{:S(2)}, u32[]{:S(2)}) %all-to-all-start.1) | async-done | bytes 1048608 | tf_op jit(solution)/shard_map/all_to_all | solution.py:155
  161.1 11.9 %scatter_custom_fusion.1 = f32[512,256]{1,0:T(8,128)S(1)} fusion(s32[2048]{0:T(1024)} %reshape.174, bf16[2048,256]{1,0:T(8,128)(2,1)S(1)} %bitcast.146, f32[]{:T(128)} %constant.108.clone.1), kind=kCustom, calls=%fused_computation.84 | custom fusion | flops 1048576 | bytes 1573376 | tf_op jit(solution)/shard_map/scatter-add | solution.py:196
  173.9 2.1 fusion.85
  177.0 7.5 %gather_fusion.2 = bf16[2048,256]{1,0:T(8,128)(2,1)S(1)} fusion(bf16[512,256]{1,0:T(8,128)(2,1)S(1)} %convolution_convert_fusion, s32[2048]{0:T(1024)S(1)} %broadcast_clamp_fusion), kind=kCustom, calls=%fused_computation.2.clone | custom fusion | bytes 2105344 | tf_op jit(solution)/shard_map/jit(_take)/gather | solution.py:210
  185.7 4.9 all-to-all-start.2
  192.7 1.5 bitcast_convert_fusion.3
  194.2 2.1 slice.91
  196.4 1.8 pad_maximum_fusion.1
  200.7 18.2 %all-to-all-done.2 = bf16[32,64,256]{2,1,0:T(8,128)(2,1)S(1)} async-done(((bf16[32,64,256]{2,1,0:T(8,128)(2,1)}), bf16[32,64,256]{2,1,0:T(8,128)(2,1)S(1)}, u32[]{:S(2)}, u32[]{:S(2)}) %all-to-all-start.2) | async-done | bytes 1048608 | tf_op jit(solution)/shard_map/all_to_all | solution.py:155
  218.9 12.9 %gather_fusion.3 = bf16[3072,256]{1,0:T(8,128)(2,1)} fusion(bf16[2048,256]{1,0:T(8,128)(2,1)S(1)} %bitcast.136, s32[3072]{0:T(1024)S(1)} %copy-done.32), kind=kCustom, calls=%fused_computation.3.clone | custom fusion | bytes 3158016 | tf_op jit(solution)/shard_map/jit(_take)/gather | solution.py:212
  231.9 4.1 convert_multiply_fusion
  236.0 2.1 broadcast.84
  238.1 176.1 %while.36 = (s32[]{:T(128)}, f32[128,256]{1,0:T(8,128)S(1)}, f32[256,768]{1,0:T(8,128)S(1)}, f32[256,768]{1,0:T(8,128)S(1)}, f32[768]{0:T(1024)S(1)}, /*index=5*...) while((s32[]{:T(128)}, f32[128,256]{1,0:T(8,128)S(1)}, ...), condition=%wide.region_6.9_spmd.clone, body=%wide.region_4.8_spmd.clone.sunk | while | flops 306152320 | bytes 12996093 | solution.py:108
  242.0 1.3 convolution_add_fusion.15
  249.3 1.3 convolution_add_fusion.15
  256.7 1.3 convolution_add_fusion.15
  264.0 1.3 convolution_add_fusion.15
  271.3 1.3 convolution_add_fusion.15
  278.6 1.3 convolution_add_fusion.15
  286.0 1.3 convolution_add_fusion.15
  293.3 1.3 convolution_add_fusion.15
  300.7 1.3 convolution_add_fusion.15
  308.0 1.3 convolution_add_fusion.15
  315.3 1.3 convolution_add_fusion.15
  352.0 1.3 convolution_add_fusion.15
  366.7 1.3 convolution_add_fusion.15
  381.4 1.3 convolution_add_fusion.15
  388.7 1.3 convolution_add_fusion.15
  396.0 1.3 convolution_add_fusion.15
  403.4 1.3 convolution_add_fusion.15
  415.5 1.5 slice.215
  417.0 17.9 %scatter_custom_fusion.2 = f32[2048,256]{1,0:T(8,128)S(1)} fusion(s32[3072]{0:T(1024)} %bitcast.154, f32[3072,256]{1,0:T(8,128)} %bitcast.147, f32[]{:T(128)} %constant.108.clone.1), kind=kCustom, calls=%fused_computation.100 | custom fusion | flops 786432 | bytes 2097664 | tf_op jit(solution)/shard_map/scatter-add | solution.py:220
  436.0 5.1 all-to-all-start.3
  442.4 76.8 %all-reduce = (f32[768]{0:T(1024)S(1)}, f32[256]{0:T(256)S(1)}, f32[256]{0:T(256)S(1)}) all-reduce(f32[768]{0:T(1024)S(1)} %get-tuple-element.357, f32[256]{0:T(256)S(1)} %copy-done.39, f32[256]{0:T(256)S(1)} %fusion.64), channel_id=1, replica_groups=mesh['replica'=8,'outer'=4,'link'=8] {'replica','outer','link'}, use_global_device_ids=true, to_apply=%region_11.14 | all-reduce | flops 1280 | bytes 10240 | tf_op jit(solution)/shard_map/psum | solution.py:231
  520.9 160.5 %all-reduce.4.cloned.1.call-done = (f32[256,768]{1,0:T(8,128)}, f32[256,768]{1,0:T(8,128)}, f32[512,256]{1,0:T(8,128)}, f32[256,256]{1,0:T(8,128)}) async-done(((f32[256,768]{1,0:T(8,128)}, f32[256,768]{1,0:T(8,128)}, f32[512,256]{1,0:T(8,128)}, f32[256,256]{1,0:T(8,128)}), (f32[256,768]{1,0:T(8,128)}, f32[256,768]{1,0:T(8,128)}, f32[512,256]{1,0:T(8,128)}, ...) | async-done | bytes 2359312 | tf_op jit(solution)/shard_map/psum | solution.py:231
  681.5 1.8 broadcast_multiply_fusion.4
  683.3 1.9 broadcast_multiply_fusion.3
  687.1 12.0 %scatter_custom_fusion.3 = f32[512,256]{1,0:T(8,128)S(1)} fusion(f32[512,256]{1,0:T(8,128)S(1)} %convolution_add_fusion.5, s32[2048]{0:T(1024)} %reshape.174, bf16[2048,256]{1,0:T(8,128)(2,1)S(1)} %bitcast.145), kind=kCustom, calls=%fused_computation.82 | custom fusion | flops 1048576 | bytes 1572864 | tf_op jit(solution)/shard_map/scatter-add | solution.py:226
  (535 shorter events, 204.2 us)
Async XLA Ops:
  7.2 166.7 %copy-start = (bf16[256,256]{1,0:T(8,128)(2,1)S(1)}, bf16[256,256]{1,0:T(8,128)(2,1)}, u32[]{:S(2)}) copy-start(bf16[256,256]{1,0:T(8,128)(2,1)} %param.36) | copy-start | bytes 393220
  16.4 12.8 %copy-start.34 = (s32[1,128,24]{1,2,0:T(8,128)S(1)}, s32[1,128,24]{1,2,0:T(8,128)}, u32[]{:S(2)}) copy-start(s32[1,128,24]{1,2,0:T(8,128)} %param.25) | copy-start | bytes 36868
  16.4 12.8 %copy-start.40 = (s32[1,128]{1,0:T(1,128)S(1)}, s32[1,128]{1,0:T(1,128)}, u32[]{:S(2)}) copy-start(s32[1,128]{1,0:T(1,128)} %param.26) | copy-start | bytes 1540
  16.4 12.8 %copy-start.33 = (bf16[1,128,256]{2,1,0:T(8,128)(2,1)S(1)}, bf16[1,128,256]{2,1,0:T(8,128)(2,1)}, u32[]{:S(2)}) copy-start(bf16[1,128,256]{2,1,0:T(8,128)(2,1)} %param.24) | copy-start | bytes 196612
  17.7 40.1 %all-to-all-start = ((bf16[32,64,256]{2,1,0:T(8,128)(2,1)}), bf16[32,64,256]{2,1,0:T(8,128)(2,1)S(1)}, u32[]{:S(2)}, u32[]{:S(2)}) async-start(bf16[32,64,256]{2,1,0:T(8,128)(2,1)} %broadcast_select_fusion.2), calls=%async_computation | async-start | bytes 2097152 | tf_op jit(solution)/shard_map/all_to_all | solution.py:155
  29.2 41.6 %copy-start.31 = (s32[3072]{0:T(1024)}, s32[3072]{0:T(1024)S(1)}, u32[]{:S(2)}) copy-start(s32[3072]{0:T(1024)S(1)} %bitcast_clamp_fusion) | copy-start | bytes 36868
  29.2 41.5 %copy-start.35 = (pred[24,128]{1,0:T(8,128)(4,1)}, pred[24,128]{1,0:T(8,128)(4,1)S(1)}, u32[]{:S(2)}) copy-start(pred[24,128]{1,0:T(8,128)(4,1)S(1)} %get-tuple-element.474) | copy-start | bytes 9220
  104.0 4.6 copy-start.12
  104.0 4.6 copy-start.29
  126.5 8.8 %copy-start.1 = (bf16[1,512,256]{2,1,0:T(8,128)(2,1)S(1)}, bf16[1,512,256]{2,1,0:T(8,128)(2,1)}, u32[]{:S(2)}) copy-start(bf16[1,512,256]{2,1,0:T(8,128)(2,1)} %param.23) | copy-start | bytes 786436
  126.5 8.8 %copy-start.13 = (bf16[512,256]{1,0:T(8,128)(2,1)S(1)}, bf16[512,256]{1,0:T(8,128)(2,1)}, u32[]{:S(2)}) copy-start(bf16[512,256]{1,0:T(8,128)(2,1)} %param.34) | copy-start | bytes 786436
  127.6 5.8 copy-start.28
  127.6 7.1 %copy-start.38 = (s32[1,512]{1,0:T(1,128)S(1)}, s32[1,512]{1,0:T(1,128)}, u32[]{:S(2)}) copy-start(s32[1,512]{1,0:T(1,128)} %param.27) | copy-start | bytes 6148
  127.6 45.4 %copy-start.14 = (bf16[512,256]{1,0:T(8,128)(2,1)S(1)}, bf16[512,256]{1,0:T(8,128)(2,1)}, u32[]{:S(2)}) copy-start(bf16[512,256]{1,0:T(8,128)(2,1)} %param.34) | copy-start | bytes 786436
  127.6 33.5 %all-to-all-start.1 = ((bf16[32,64,256]{2,1,0:T(8,128)(2,1)}), bf16[32,64,256]{2,1,0:T(8,128)(2,1)S(1)}, u32[]{:S(2)}, u32[]{:S(2)}) async-start(bf16[32,64,256]{2,1,0:T(8,128)(2,1)} %bitcast.142), calls=%async_computation.1 | async-start | bytes 2097152 | tf_op jit(solution)/shard_map/all_to_all | solution.py:155
  185.7 33.2 %all-to-all-start.2 = ((bf16[32,64,256]{2,1,0:T(8,128)(2,1)}), bf16[32,64,256]{2,1,0:T(8,128)(2,1)S(1)}, u32[]{:S(2)}, u32[]{:S(2)}) async-start(bf16[32,64,256]{2,1,0:T(8,128)(2,1)} %broadcast_select_fusion.1), calls=%async_computation.2 | async-start | bytes 2097152 | tf_op jit(solution)/shard_map/all_to_all | solution.py:155
  190.6 490.8 %all-reduce.4.cloned.1.call-start = ((), (), s32[]{:S(2)}) async-start(), calls=%async_computation.4 | async-start | bytes 4718592 | tf_op jit(solution)/shard_map/psum | solution.py:231
  198.8 20.2 %copy-start.32 = (s32[3072]{0:T(1024)S(1)}, s32[3072]{0:T(1024)}, u32[]{:S(2)}) copy-start(s32[3072]{0:T(1024)} %copy-done.31) | copy-start | bytes 36868
  218.9 12.9 %copy-start.30 = (f32[24,128]{1,0:T(8,128)S(1)}, f32[24,128]{1,0:T(8,128)}, u32[]{:S(2)}) copy-start(f32[24,128]{1,0:T(8,128)} %copy-done.29) | copy-start | bytes 36868
  218.9 13.0 %copy-start.36 = (pred[24,128]{1,0:T(8,128)(4,1)S(1)}, pred[24,128]{1,0:T(8,128)(4,1)}, u32[]{:S(2)}) copy-start(pred[24,128]{1,0:T(8,128)(4,1)} %copy-done.35) | copy-start | bytes 9220
  239.2 2.4 copy-start.27
  246.6 2.4 copy-start.27
  253.9 2.4 copy-start.27
  268.6 2.4 copy-start.27
  283.2 2.4 copy-start.27
  290.6 2.4 copy-start.27
  297.9 2.4 copy-start.27
  312.6 2.4 copy-start.27
  319.9 2.4 copy-start.27
  334.6 2.4 copy-start.27
  341.9 2.4 copy-start.27
  349.3 2.4 copy-start.27
  356.6 2.4 copy-start.27
  363.9 2.4 copy-start.27
  371.3 2.4 copy-start.27
  378.6 2.4 copy-start.27
  385.9 2.4 copy-start.27
  393.3 2.4 copy-start.27
  400.6 2.4 copy-start.27
  407.9 2.4 copy-start.27
  414.1 20.8 %copy-start.8 = (f32[128,256]{1,0:T(8,128)}, f32[128,256]{1,0:T(8,128)S(1)}, u32[]{:S(2)}) copy-start(f32[128,256]{1,0:T(8,128)S(1)} %get-tuple-element.354) | copy-start | bytes 393220
  434.9 6.2 copy-start.41
  436.0 5.1 copy-start.22
  436.0 6.1 copy-start.11
  436.0 6.1 copy-start.15
  436.0 251.0 %all-to-all-start.3 = ((bf16[32,64,256]{2,1,0:T(8,128)(2,1)}), bf16[32,64,256]{2,1,0:T(8,128)(2,1)S(1)}, u32[]{:S(2)}, u32[]{:S(2)}) async-start(bf16[32,64,256]{2,1,0:T(8,128)(2,1)} %bitcast.141), calls=%async_computation.3 | async-start | bytes 2097152 | tf_op jit(solution)/shard_map/all_to_all | solution.py:155
  681.5 3.7 copy-start.19
  681.5 4.6 copy-start.18
  (22 other events, 38.1 us)
Sparse Core Ops, SparseCore 0:
  415.4 265.9 all-reduce.3
where the time goes:
time: 711 us; the launch traced here: 707 us
  waiting for transfers between devices  232 us (33%)
  matrix products  158 us (22%)
  other arithmetic  141 us (20%)
  blocking collectives  76.8 us (11%)
  local copies, waits for them, and re-layouts  54.8 us (8%)
  starting transfers between devices  26.9 us (4%)
  between operations  14.5 us (2%)
    psum x1, waiting for transfers between devices, body(): lax.psum((finished[1], finished[2], finished[3], mlp_terms[0], mlp_terms[...  161 us
    psum x1, blocking collectives, body(): lax.psum((finished[1], finished[2], finished[3], mlp_terms[0], mlp_terms[...  76.8 us
    all_to_all x4, waiting for transfers between devices, swap_slots(): lax.all_to_all(blocks, ('outer', 'link'), split_axis=0, concat_axis=0, ti...  71.6 us
    dot_general x48, matrix products, gate_terms(): jnp.dot(hop_input, input_weight, preferred_element_type=jnp.float32)  31.8 us
    dot_general x48, matrix products, gate_terms(): jnp.dot(state_now.astype(jnp.bfloat16), hidden_weight, preferred_element_...  31.7 us
    dot_general x24, matrix products, back_step(): jnp.dot(state_now.astype(jnp.bfloat16).T, hid_bf, preferred_element_type=...  31 us
    dot_general x24, matrix products, back_step(): jnp.dot(hop_input.T, in_bf, preferred_element_type=jnp.float32)  29.4 us
    all_to_all x4, starting transfers between devices, swap_slots(): lax.all_to_all(blocks, ('outer', 'link'), split_axis=0, concat_axis=0, ti...  26.7 us
  transfers between devices with their start and end apart: 5, of which 4 were waited for; matrix products, arithmetic and copies ran while one was open for 6% of the time, Pallas kernels for 0%

commit v1 on v0

--- a/solution.py
+++ b/solution.py
@@ -228,7 +228,7 @@
         serve_flat,
         num_segments=link_count,
     )
-    summed = lax.psum(
+    inner = lax.psum(
         (
             finished[1],
             finished[2],
@@ -238,8 +238,9 @@
             mlp_terms[2],
             mlp_terms[3],
         ),
-        ("replica", "outer", "link"),
-    )
+        "replica",
+    )
+    summed = lax.psum(inner, ("outer", "link"))
     device_count = lax.axis_size("replica") * lax.axis_size("outer") * lax.axis_size("link")
     grad_scale = float(device_count * link_count) ** (-0.5)
     return (

time: 711 us -> 675 us (0.949)
  waiting for transfers between devices: 232 us -> 174 us
  blocking collectives: 76.8 us -> 95.8 us
    psum x1, waiting for transfers between devices: 161 us -> 65.9 us  [body(): lax.psum((finished[1], finished[2], finished[3], mlp_terms[0], mlp_terms[...]
    psum x0 -> x1, blocking collectives: none -> 82.1 us  [body(): summed = lax.psum(inner, ('outer', 'link'))]
    psum x1, blocking collectives: 76.8 us -> 13.7 us  [body(): lax.psum((finished[1], finished[2], finished[3], mlp_terms[0], mlp_terms[...]
    psum x0 -> x1, waiting for transfers between devices: none -> 36.1 us  [body(): summed = lax.psum(inner, ('outer', 'link'))]
  transfers between devices with their start and end apart: 5 -> 6, of which waited for: 4 -> 5; matrix products, arithmetic and copies ran while one was open for 6% -> 7% of each run, Pallas kernels for 0% -> 0%
where the time goes in v1:
time: 675 us; the launch traced here: 671 us
  waiting for transfers between devices  174 us (26%)
  matrix products  158 us (23%)
  other arithmetic  141 us (21%)
  blocking collectives  95.8 us (14%)
  local copies, waits for them, and re-layouts  54 us (8%)
  starting transfers between devices  31.9 us (5%)
  between operations  14.5 us (2%)
    psum x1, blocking collectives, body(): summed = lax.psum(inner, ('outer', 'link'))  82.1 us
    all_to_all x4, waiting for transfers between devices, swap_slots(): lax.all_to_all(blocks, ('outer', 'link'), split_axis=0, concat_axis=0, ti...  71.7 us
    psum x1, waiting for transfers between devices, body(): lax.psum((finished[1], finished[2], finished[3], mlp_terms[0], mlp_terms[...  65.9 us
    psum x1, waiting for transfers between devices, body(): summed = lax.psum(inner, ('outer', 'link'))  36.1 us
    dot_general x48, matrix products, gate_terms(): jnp.dot(hop_input, input_weight, preferred_element_type=jnp.float32)  31.8 us
    dot_general x48, matrix products, gate_terms(): jnp.dot(state_now.astype(jnp.bfloat16), hidden_weight, preferred_element_...  31.7 us
    all_to_all x4, starting transfers between devices, swap_slots(): lax.all_to_all(blocks, ('outer', 'link'), split_axis=0, concat_axis=0, ti...  31.6 us
    dot_general x24, matrix products, back_step(): jnp.dot(state_now.astype(jnp.bfloat16).T, hid_bf, preferred_element_type=...  31 us
  transfers between devices with their start and end apart: 6, of which 5 were waited for; matrix products, arithmetic and copies ran while one was open for 7% of the time, Pallas kernels for 0%

profile of v1, /device:TPU:2, one launch (start us, length us, event | category | flops | bytes accessed | tf_op | source)
XLA Modules:
  0.0 671.5 jit_solution(14594991080161460262)
XLA Ops:
  8.8 7.6 %gather_fusion = bf16[2048,256]{1,0:T(8,128)(2,1)S(1)} fusion(bf16[512,256]{1,0:T(8,128)(2,1)} %bitcast.135, s32[2048]{0:T(1024)S(1)} %broadcast_clamp_fusion), kind=kCustom, calls=%fused_computation.clone | custom fusion | bytes 2105344 | tf_op jit(solution)/shard_map/jit(_take)/gather | solution.py:187
  17.7 11.5 %all-to-all-start = ((bf16[32,64,256]{2,1,0:T(8,128)(2,1)}), bf16[32,64,256]{2,1,0:T(8,128)(2,1)S(1)}, u32[]{:S(2)}, u32[]{:S(2)}) async-start(bf16[32,64,256]{2,1,0:T(8,128)(2,1)} %broadcast_select_fusion.2), calls=%async_computation | async-start | bytes 2097152 | tf_op jit(solution)/shard_map/all_to_all | solution.py:155
  29.9 27.9 %all-to-all-done = bf16[32,64,256]{2,1,0:T(8,128)(2,1)S(1)} async-done(((bf16[32,64,256]{2,1,0:T(8,128)(2,1)}), bf16[32,64,256]{2,1,0:T(8,128)(2,1)S(1)}, u32[]{:S(2)}, u32[]{:S(2)}) %all-to-all-start) | async-done | bytes 1048608 | tf_op jit(solution)/shard_map/all_to_all | solution.py:155
  57.8 13.0 %gather_fusion.1 = bf16[3072,256]{1,0:T(8,128)(2,1)} fusion(bf16[2048,256]{1,0:T(8,128)(2,1)S(1)} %bitcast.137, s32[3072]{0:T(1024)S(1)} %bitcast_clamp_fusion), kind=kCustom, calls=%fused_computation.1.clone | custom fusion | bytes 3158016 | tf_op jit(solution)/shard_map/jit(_take)/gather | solution.py:188
  70.7 1.7 broadcast_select_fusion
  72.5 2.0 broadcast.84.clone
  74.6 29.4 %while.35 = (s32[]{:T(128)}, f32[128,256]{1,0:T(8,128)S(1)}, f32[24,128,256]{2,1,0:T(8,128)}, f32[24,128]{1,0:T(8,128)S(1)}, bf16[24,128,256]{2,1,0:T(8,128)(2,1...) while((s32[]{:T(128)}, f32[128,256]{1,0:T(8,128)S(1)}, ...), condition=%wide.region_1.4_spmd, body=%wide.region_0.3_spmd.sunk | while | flops 101253248 | bytes 2954097 | solution.py:36
  104.0 4.6 broadcast_multiply_fusion
  108.5 17.9 %scatter_custom_fusion = f32[2048,256]{1,0:T(8,128)S(1)} fusion(s32[3072]{0:T(1024)S(1)} %bitcast.155, f32[3072,256]{1,0:T(8,128)} %bitcast.148, f32[]{:T(128)} %constant.108.clone.1), kind=kCustom, calls=%fused_computation.102 | custom fusion | flops 786432 | bytes 2097664 | tf_op jit(solution)/shard_map/scatter-add | solution.py:190
  127.6 5.2 all-to-all-start.1
  135.5 25.6 %all-to-all-done.1 = bf16[32,64,256]{2,1,0:T(8,128)(2,1)S(1)} async-done(((bf16[32,64,256]{2,1,0:T(8,128)(2,1)}), bf16[32,64,256]{2,1,0:T(8,128)(2,1)S(1)}, u32[]{:S(2)}, u32[]{:S(2)}) %all-to-all-start.1) | async-done | bytes 1048608 | tf_op jit(solution)/shard_map/all_to_all | solution.py:155
  161.1 11.9 %scatter_custom_fusion.1 = f32[512,256]{1,0:T(8,128)S(1)} fusion(s32[2048]{0:T(1024)} %reshape.174, bf16[2048,256]{1,0:T(8,128)(2,1)S(1)} %bitcast.146, f32[]{:T(128)} %constant.108.clone.1), kind=kCustom, calls=%fused_computation.84 | custom fusion | flops 1048576 | bytes 1573376 | tf_op jit(solution)/shard_map/scatter-add | solution.py:196
  173.9 2.1 fusion.85
  177.0 7.5 %gather_fusion.2 = bf16[2048,256]{1,0:T(8,128)(2,1)S(1)} fusion(bf16[512,256]{1,0:T(8,128)(2,1)S(1)} %convolution_convert_fusion, s32[2048]{0:T(1024)S(1)} %broadcast_clamp_fusion), kind=kCustom, calls=%fused_computation.2.clone | custom fusion | bytes 2105344 | tf_op jit(solution)/shard_map/jit(_take)/gather | solution.py:210
  185.7 4.9 all-to-all-start.2
  192.7 1.5 bitcast_convert_fusion.3
  194.2 2.1 slice.91
  196.3 1.8 pad_maximum_fusion.1
  200.7 18.2 %all-to-all-done.2 = bf16[32,64,256]{2,1,0:T(8,128)(2,1)S(1)} async-done(((bf16[32,64,256]{2,1,0:T(8,128)(2,1)}), bf16[32,64,256]{2,1,0:T(8,128)(2,1)S(1)}, u32[]{:S(2)}, u32[]{:S(2)}) %all-to-all-start.2) | async-done | bytes 1048608 | tf_op jit(solution)/shard_map/all_to_all | solution.py:155
  218.9 12.9 %gather_fusion.3 = bf16[3072,256]{1,0:T(8,128)(2,1)} fusion(bf16[2048,256]{1,0:T(8,128)(2,1)S(1)} %bitcast.136, s32[3072]{0:T(1024)S(1)} %copy-done.32), kind=kCustom, calls=%fused_computation.3.clone | custom fusion | bytes 3158016 | tf_op jit(solution)/shard_map/jit(_take)/gather | solution.py:212
  231.9 4.1 convert_multiply_fusion
  236.0 2.1 broadcast.84
  238.1 176.1 %while.36 = (s32[]{:T(128)}, f32[128,256]{1,0:T(8,128)S(1)}, f32[256,768]{1,0:T(8,128)S(1)}, f32[256,768]{1,0:T(8,128)S(1)}, f32[768]{0:T(1024)S(1)}, /*index=5*...) while((s32[]{:T(128)}, f32[128,256]{1,0:T(8,128)S(1)}, ...), condition=%wide.region_6.9_spmd.clone, body=%wide.region_4.8_spmd.clone.sunk | while | flops 306152320 | bytes 12996093 | solution.py:108
  242.0 1.3 convolution_add_fusion.15
  249.3 1.3 convolution_add_fusion.15
  256.7 1.3 convolution_add_fusion.15
  264.0 1.3 convolution_add_fusion.15
  271.3 1.3 convolution_add_fusion.15
  286.0 1.3 convolution_add_fusion.15
  293.3 1.3 convolution_add_fusion.15
  300.7 1.3 convolution_add_fusion.15
  315.3 1.3 convolution_add_fusion.15
  352.0 1.3 convolution_add_fusion.15
  366.7 1.3 convolution_add_fusion.15
  381.4 1.3 convolution_add_fusion.15
  388.7 1.3 convolution_add_fusion.15
  396.0 1.3 convolution_add_fusion.15
  403.4 1.3 convolution_add_fusion.15
  415.4 65.9 %all-reduce.9.cloned.1.call-done = (f32[256,768]{1,0:T(8,128)}, f32[256,768]{1,0:T(8,128)}, f32[512,256]{1,0:T(8,128)}, f32[256,256]{1,0:T(8,128)}) async-done(((f32[256,768]{1,0:T(8,128)}, f32[256,768]{1,0:T(8,128)}, f32[512,256]{1,0:T(8,128)}, f32[256,256]{1,0:T(8,128)}), (f32[256,768]{1,0:T(8,128)}, f32[256,768]{1,0:T(8,128)}, f32[512,256]{1,0:T(8,128)}, ...) | async-done | bytes 2359312 | tf_op jit(solution)/shard_map/psum | solution.py:231
  481.3 17.9 %scatter_custom_fusion.2 = f32[2048,256]{1,0:T(8,128)S(1)} fusion(s32[3072]{0:T(1024)} %bitcast.154, f32[3072,256]{1,0:T(8,128)} %bitcast.147, f32[]{:T(128)} %constant.108.clone.1), kind=kCustom, calls=%fused_computation.100 | custom fusion | flops 786432 | bytes 2097664 | tf_op jit(solution)/shard_map/scatter-add | solution.py:220
  500.3 10.0 %all-to-all-start.3 = ((bf16[32,64,256]{2,1,0:T(8,128)(2,1)}), bf16[32,64,256]{2,1,0:T(8,128)(2,1)S(1)}, u32[]{:S(2)}, u32[]{:S(2)}) async-start(bf16[32,64,256]{2,1,0:T(8,128)(2,1)} %bitcast.141), calls=%async_computation.3 | async-start | bytes 2097152 | tf_op jit(solution)/shard_map/all_to_all | solution.py:155
  510.5 1.5 slice.215
  513.3 13.7 %all-reduce.2 = (f32[768]{0:T(1024)S(1)}, f32[256]{0:T(256)S(1)}, f32[256]{0:T(256)S(1)}) all-reduce(f32[768]{0:T(1024)S(1)} %get-tuple-element.357, f32[256]{0:T(256)S(1)} %copy-done.39, f32[256]{0:T(256)S(1)} %fusion.64), channel_id=1, replica_groups=mesh['replica'=8,'outer'=4,'link'=8] {'replica'}, use_global_device_ids=true, to_apply=%region_13.16 | all-reduce | flops 1280 | bytes 10240 | tf_op jit(solution)/shard_map/psum | solution.py:231
  527.0 82.1 %all-reduce = (f32[768]{0:T(1024)S(1)}, f32[256]{0:T(256)S(1)}, f32[256]{0:T(256)S(1)}) all-reduce(f32[768]{0:T(1024)S(1)} %get-tuple-element.459, f32[256]{0:T(256)S(1)} %get-tuple-element.460, f32[256]{0:T(256)S(1)} %get-tuple-element.461), channel_id=1, replica_groups=mesh['replica'=8,'outer'=4,'link'=8] {'outer','link'}, use_global_device_ids=true, to_apply=%region_14.17 | all-reduce | flops 1280 | bytes 10240 | tf_op jit(solution)/shard_map/psum | solution.py:243
  610.9 12.0 %scatter_custom_fusion.3 = f32[512,256]{1,0:T(8,128)S(1)} fusion(f32[512,256]{1,0:T(8,128)S(1)} %convolution_add_fusion.5, s32[2048]{0:T(1024)} %reshape.174, bf16[2048,256]{1,0:T(8,128)(2,1)S(1)} %bitcast.145), kind=kCustom, calls=%fused_computation.82 | custom fusion | flops 1048576 | bytes 1572864 | tf_op jit(solution)/shard_map/scatter-add | solution.py:226
  622.8 36.1 %all-reduce.7.cloned.1.call-done = (f32[256,768]{1,0:T(8,128)}, f32[256,768]{1,0:T(8,128)}, f32[512,256]{1,0:T(8,128)}, f32[256,256]{1,0:T(8,128)}) async-done(((f32[256,768]{1,0:T(8,128)}, f32[256,768]{1,0:T(8,128)}, f32[512,256]{1,0:T(8,128)}, f32[256,256]{1,0:T(8,128)}), (f32[256,768]{1,0:T(8,128)}, f32[256,768]{1,0:T(8,128)}, f32[512,256]{1,0:T(8,128)}, ...) | async-done | bytes 2359312 | tf_op jit(solution)/shard_map/psum | solution.py:243
  659.0 2.2 broadcast_multiply_fusion.2
  661.2 1.7 broadcast_multiply_fusion.4
  (539 shorter events, 205.9 us)
Async XLA Ops:
  7.2 166.7 %copy-start = (bf16[256,256]{1,0:T(8,128)(2,1)S(1)}, bf16[256,256]{1,0:T(8,128)(2,1)}, u32[]{:S(2)}) copy-start(bf16[256,256]{1,0:T(8,128)(2,1)} %param.36) | copy-start | bytes 393220
  16.4 12.8 %copy-start.34 = (s32[1,128,24]{1,2,0:T(8,128)S(1)}, s32[1,128,24]{1,2,0:T(8,128)}, u32[]{:S(2)}) copy-start(s32[1,128,24]{1,2,0:T(8,128)} %param.25) | copy-start | bytes 36868
  16.4 12.8 %copy-start.40 = (s32[1,128]{1,0:T(1,128)S(1)}, s32[1,128]{1,0:T(1,128)}, u32[]{:S(2)}) copy-start(s32[1,128]{1,0:T(1,128)} %param.26) | copy-start | bytes 1540
  16.4 12.8 %copy-start.33 = (bf16[1,128,256]{2,1,0:T(8,128)(2,1)S(1)}, bf16[1,128,256]{2,1,0:T(8,128)(2,1)}, u32[]{:S(2)}) copy-start(bf16[1,128,256]{2,1,0:T(8,128)(2,1)} %param.24) | copy-start | bytes 196612
  17.7 40.1 %all-to-all-start = ((bf16[32,64,256]{2,1,0:T(8,128)(2,1)}), bf16[32,64,256]{2,1,0:T(8,128)(2,1)S(1)}, u32[]{:S(2)}, u32[]{:S(2)}) async-start(bf16[32,64,256]{2,1,0:T(8,128)(2,1)} %broadcast_select_fusion.2), calls=%async_computation | async-start | bytes 2097152 | tf_op jit(solution)/shard_map/all_to_all | solution.py:155
  29.2 41.6 %copy-start.31 = (s32[3072]{0:T(1024)}, s32[3072]{0:T(1024)S(1)}, u32[]{:S(2)}) copy-start(s32[3072]{0:T(1024)S(1)} %bitcast_clamp_fusion) | copy-start | bytes 36868
  29.2 41.5 %copy-start.35 = (pred[24,128]{1,0:T(8,128)(4,1)}, pred[24,128]{1,0:T(8,128)(4,1)S(1)}, u32[]{:S(2)}) copy-start(pred[24,128]{1,0:T(8,128)(4,1)S(1)} %get-tuple-element.481) | copy-start | bytes 9220
  104.0 4.6 copy-start.12
  104.0 4.6 copy-start.29
  126.5 8.8 %copy-start.1 = (bf16[1,512,256]{2,1,0:T(8,128)(2,1)S(1)}, bf16[1,512,256]{2,1,0:T(8,128)(2,1)}, u32[]{:S(2)}) copy-start(bf16[1,512,256]{2,1,0:T(8,128)(2,1)} %param.23) | copy-start | bytes 786436
  126.5 8.8 %copy-start.13 = (bf16[512,256]{1,0:T(8,128)(2,1)S(1)}, bf16[512,256]{1,0:T(8,128)(2,1)}, u32[]{:S(2)}) copy-start(bf16[512,256]{1,0:T(8,128)(2,1)} %param.34) | copy-start | bytes 786436
  127.6 5.8 copy-start.28
  127.6 7.1 %copy-start.38 = (s32[1,512]{1,0:T(1,128)S(1)}, s32[1,512]{1,0:T(1,128)}, u32[]{:S(2)}) copy-start(s32[1,512]{1,0:T(1,128)} %param.27) | copy-start | bytes 6148
  127.6 45.4 %copy-start.14 = (bf16[512,256]{1,0:T(8,128)(2,1)S(1)}, bf16[512,256]{1,0:T(8,128)(2,1)}, u32[]{:S(2)}) copy-start(bf16[512,256]{1,0:T(8,128)(2,1)} %param.34) | copy-start | bytes 786436
  127.6 33.5 %all-to-all-start.1 = ((bf16[32,64,256]{2,1,0:T(8,128)(2,1)}), bf16[32,64,256]{2,1,0:T(8,128)(2,1)S(1)}, u32[]{:S(2)}, u32[]{:S(2)}) async-start(bf16[32,64,256]{2,1,0:T(8,128)(2,1)} %bitcast.142), calls=%async_computation.1 | async-start | bytes 2097152 | tf_op jit(solution)/shard_map/all_to_all | solution.py:155
  185.7 33.2 %all-to-all-start.2 = ((bf16[32,64,256]{2,1,0:T(8,128)(2,1)}), bf16[32,64,256]{2,1,0:T(8,128)(2,1)S(1)}, u32[]{:S(2)}, u32[]{:S(2)}) async-start(bf16[32,64,256]{2,1,0:T(8,128)(2,1)} %broadcast_select_fusion.1), calls=%async_computation.2 | async-start | bytes 2097152 | tf_op jit(solution)/shard_map/all_to_all | solution.py:155
  190.6 290.6 %all-reduce.9.cloned.1.call-start = ((), (), s32[]{:S(2)}) async-start(), calls=%async_computation.5 | async-start | bytes 4718592 | tf_op jit(solution)/shard_map/psum | solution.py:231
  198.7 20.2 %copy-start.32 = (s32[3072]{0:T(1024)S(1)}, s32[3072]{0:T(1024)}, u32[]{:S(2)}) copy-start(s32[3072]{0:T(1024)} %copy-done.31) | copy-start | bytes 36868
  218.9 12.9 %copy-start.30 = (f32[24,128]{1,0:T(8,128)S(1)}, f32[24,128]{1,0:T(8,128)}, u32[]{:S(2)}) copy-start(f32[24,128]{1,0:T(8,128)} %copy-done.29) | copy-start | bytes 36868
  218.9 13.0 %copy-start.36 = (pred[24,128]{1,0:T(8,128)(4,1)S(1)}, pred[24,128]{1,0:T(8,128)(4,1)}, u32[]{:S(2)}) copy-start(pred[24,128]{1,0:T(8,128)(4,1)} %copy-done.35) | copy-start | bytes 9220
  239.2 2.4 copy-start.27
  246.6 2.4 copy-start.27
  253.9 2.4 copy-start.27
  268.6 2.4 copy-start.27
  283.2 2.4 copy-start.27
  290.6 2.4 copy-start.27
  297.9 2.4 copy-start.27
  312.6 2.4 copy-start.27
  319.9 2.4 copy-start.27
  334.6 2.4 copy-start.27
  341.9 2.4 copy-start.27
  349.3 2.4 copy-start.27
  356.6 2.4 copy-start.27
  363.9 2.4 copy-start.27
  371.3 2.4 copy-start.27
  385.9 2.4 copy-start.27
  407.9 2.4 copy-start.27
  414.1 67.1 %copy-start.8 = (f32[128,256]{1,0:T(8,128)}, f32[128,256]{1,0:T(8,128)S(1)}, u32[]{:S(2)}) copy-start(f32[128,256]{1,0:T(8,128)S(1)} %get-tuple-element.354) | copy-start | bytes 393220
  415.3 243.7 %all-reduce.7.cloned.1.call-start = ((), (), s32[]{:S(2)}) async-start(), calls=%async_computation.4 | async-start | bytes 4718592 | tf_op jit(solution)/shard_map/psum | solution.py:243
  499.2 11.1 %copy-start.17 = (bf16[1,512,256]{2,1,0:T(8,128)(2,1)S(1)}, bf16[1,512,256]{2,1,0:T(8,128)(2,1)}, u32[]{:S(2)}) copy-start(bf16[1,512,256]{2,1,0:T(8,128)(2,1)} %param.29) | copy-start | bytes 786436
  499.2 12.8 %copy-start.41 = (f32[256]{0:T(256)S(1)}, f32[256]{0:T(256)}, u32[]{:S(2)}) copy-start(f32[256]{0:T(256)} %param.37) | copy-start | bytes 3076
  500.3 11.7 %copy-start.21 = (f32[512,256]{1,0:T(8,128)S(1)}, f32[512,256]{1,0:T(8,128)}, u32[]{:S(2)}) copy-start(f32[512,256]{1,0:T(8,128)} %copy-done.19) | copy-start | bytes 1572868
  500.3 110.5 %all-to-all-start.3 = ((bf16[32,64,256]{2,1,0:T(8,128)(2,1)}), bf16[32,64,256]{2,1,0:T(8,128)(2,1)S(1)}, u32[]{:S(2)}, u32[]{:S(2)}) async-start(bf16[32,64,256]{2,1,0:T(8,128)(2,1)} %bitcast.141), calls=%async_computation.3 | async-start | bytes 2097152 | tf_op jit(solution)/shard_map/all_to_all | solution.py:155
  510.3 2.7 copy-start.11
  510.3 2.7 copy-start.15
  622.8 41.8 %copy-start.24 = (f32[512,256]{1,0:T(8,128)}, f32[512,256]{1,0:T(8,128)S(1)}, u32[]{:S(2)}) copy-start(f32[512,256]{1,0:T(8,128)S(1)} %scatter_custom_fusion.3) | copy-start | bytes 1572868
  659.0 3.9 copy-start.23
  659.0 4.7 copy-start.18
  (23 other events, 43.2 us)
Sparse Core Ops, SparseCore 0:
  415.4 65.7 all-reduce.8
  485.2 173.7 all-reduce.6
